TPU v7x, 256 devices: a whole 4x4x8 slice. The times are simulated.
256 devices in a mesh: dp: 64 (over z, y, core), section: 4 (over x).
Axes of the slice: x: 4, y: 4, z: 8, core: 2. Of those that a mesh axis runs over, the one named last changes fastest.
Arguments:
- hidden_in: bfloat16 [4, 2, 64, 4096], P('section', None, 'dp'), may hold values from -48 to 48
- grad_out: bfloat16 [2, 64, 4096], P(None, 'dp'), may hold values from -6 to 6
- weight_gate: bfloat16 [4, 14336, 4096], P('section', 'dp'), may hold values from -0.09375 to 0.09375
- weight_up: bfloat16 [4, 14336, 4096], P('section', 'dp'), may hold values from -0.09375 to 0.09375
- weight_down: bfloat16 [4, 14336, 4096], P('section', 'dp'), may hold values from -0.046875 to 0.046875
- gain: float32 [4, 4096], P('section'), may hold values from 0.5 to 1.5
- counts: int32 [2], replicated, may hold values from 1 to 64, 85 in all
Outputs:
- grad_inputs: bfloat16 [4, 2, 64, 4096], P('section', None, 'dp')
- gate_grads: bfloat16 [4, 14336, 4096], P('section', 'dp')
- up_grads: bfloat16 [4, 14336, 4096], P('section', 'dp')
- down_grads: bfloat16 [4, 14336, 4096], P('section', 'dp')
- gain_grads: float32 [4, 4096], P('section')
Inputs may be any that keep to these rules, and one draw needn't show every extreme that they name: The 2 counts sum to 85.
All inputs are finite; a program needn't handle non-finite values.
Results may differ from a plain program's by a relative error of at most 0.012.
Values may be sent and summed in bfloat16 or wider, within the bound.
No kernel may reach another device: no remote copies, remote signals or barrier semaphores. Data moves between devices by JAX's collectives and lax.ppermute only.
A program may use at most 128 MiB of HBM per device.

v0:
```python
import jax
import jax.numpy as jnp
from jax import lax
from jax.sharding import PartitionSpec as P


def from_behind(x, axis, by):
    size = lax.axis_size(axis)
    pairs = [(i, i + by) for i in range(size) if 0 <= i + by < size]
    return lax.ppermute(x, axis, pairs)


def norm_rows(layer_rows, gain_row):
    row_values = layer_rows.astype(jnp.float32)
    inv_rms = lax.rsqrt(jnp.mean(row_values * row_values, axis=-1, keepdims=True) + 1e-05)
    normed_rows = (row_values * inv_rms * gain_row).astype(jnp.bfloat16)
    return (inv_rms, normed_rows)


def unit_grads(upstream, gate_pre, up_pre, down_mat):
    sigmoid_pre = jax.nn.sigmoid(gate_pre)
    silu_pre = gate_pre * sigmoid_pre
    activation = (silu_pre * up_pre).astype(jnp.bfloat16)
    grad_act = lax.dot_general(
        upstream, down_mat, (((1,), (1,)), ((), ())), preferred_element_type=jnp.float32
    )
    grad_gate = (grad_act * up_pre * sigmoid_pre * (1.0 + gate_pre * (1.0 - sigmoid_pre))).astype(
        jnp.bfloat16
    )
    grad_up = (grad_act * silu_pre).astype(jnp.bfloat16)
    return (activation, grad_gate, grad_up)


def norm_back(layer_rows, inv_rms, upstream, grad_normed, gain_row):
    row_values = layer_rows.astype(jnp.float32)
    gained_grad = gain_row * grad_normed
    inner_sum = jnp.sum(gained_grad * row_values, axis=-1, keepdims=True)
    feature_count = row_values.shape[-1]
    grad_rows = (
        upstream.astype(jnp.float32)
        + inv_rms * gained_grad
        - row_values * inv_rms**3 * inner_sum / feature_count
    )
    return grad_rows.astype(jnp.bfloat16)


def transposed_product(left_rows, right_rows):
    return lax.dot_general(
        left_rows, right_rows, (((0,), (0,)), ((), ())), preferred_element_type=jnp.float32
    )


def pick_block(stacked, index_value):
    return lax.dynamic_index_in_dim(stacked, index_value, 0, keepdims=False)


def on_device(hidden_in, grad_out, weight_gate, weight_up, weight_down, gain, counts):
    section_count = lax.axis_size("section")
    section_pos = lax.axis_index("section")
    dp_pos = lax.axis_index("dp")
    layer_rows = hidden_in[0]
    gate_mat = weight_gate[0]
    up_mat = weight_up[0]
    down_mat = weight_down[0]
    gain_row = gain[0]
    batch_count, slot_local, feature_count = layer_rows.shape
    unit_count = gate_mat.shape[0]
    full_slots = slot_local * lax.axis_size("dp")
    slot_ids = dp_pos * slot_local + jnp.arange(slot_local)
    live_slots = slot_ids[None, :] < counts[:, None]
    top_local = jnp.where(live_slots[:, :, None], grad_out, jnp.zeros((), jnp.bfloat16))
    is_last = section_pos == section_count - 1
    top_whole = lax.all_gather(top_local, "dp", axis=1, tiled=True)
    received = jnp.zeros((full_slots, feature_count), jnp.bfloat16)
    gathered_all = lax.all_gather(layer_rows, "dp", axis=1, tiled=True)
    all_inv, all_normed = norm_rows(gathered_all, gain_row)
    all_gate = jnp.einsum("mpd,fd->mpf", all_normed, gate_mat, preferred_element_type=jnp.float32)
    all_up = jnp.einsum("mpd,fd->mpf", all_normed, up_mat, preferred_element_type=jnp.float32)
    grad_store = jnp.zeros_like(layer_rows)
    gate_total = jnp.zeros((unit_count, feature_count), jnp.float32)
    up_total = jnp.zeros((unit_count, feature_count), jnp.float32)
    down_total = jnp.zeros((unit_count, feature_count), jnp.float32)
    gain_total = jnp.zeros((feature_count,), jnp.float32)
    last_step = batch_count + section_count - 2
    for step_index in range(batch_count + section_count - 1):
        micro_index = step_index - (section_count - 1 - section_pos)
        is_valid = (micro_index >= 0) & (micro_index < batch_count)
        clamped = jnp.clip(micro_index, 0, batch_count - 1)
        gathered = pick_block(gathered_all, clamped)
        gate_pre = pick_block(all_gate, clamped)
        up_pre = pick_block(all_up, clamped)
        full_inv = pick_block(all_inv, clamped)
        full_normed = pick_block(all_normed, clamped)
        full_up = jnp.where(is_last, pick_block(top_whole, clamped), received)
        full_up = jnp.where(is_valid, full_up, jnp.zeros((), jnp.bfloat16))
        activation, grad_gate, grad_up = unit_grads(full_up, gate_pre, up_pre, down_mat)
        gate_total = gate_total + transposed_product(grad_gate, full_normed)
        up_total = up_total + transposed_product(grad_up, full_normed)
        down_total = down_total + transposed_product(activation, full_up)
        partial_sum = jnp.dot(grad_gate, gate_mat, preferred_element_type=jnp.float32) + jnp.dot(
            grad_up, up_mat, preferred_element_type=jnp.float32
        )
        grad_normed = lax.psum(partial_sum, "dp")
        grad_full = norm_back(gathered, full_inv, full_up, grad_normed, gain_row)
        gain_total = gain_total + jnp.sum(
            grad_normed * gathered.astype(jnp.float32) * full_inv, axis=0
        )
        grad_own = lax.dynamic_slice_in_dim(grad_full, dp_pos * slot_local, slot_local, 0)
        old_rows = pick_block(grad_store, clamped)
        grad_store = lax.dynamic_update_index_in_dim(
            grad_store, jnp.where(is_valid, grad_own, old_rows), clamped, 0
        )
        if step_index < last_step:
            received = from_behind(grad_full, "section", -1)
    return (
        grad_store[None],
        gate_total.astype(jnp.bfloat16)[None],
        up_total.astype(jnp.bfloat16)[None],
        down_total.astype(jnp.bfloat16)[None],
        gain_total[None],
    )


def solution(mesh):
    return jax.shard_map(
        on_device,
        mesh=mesh,
        in_specs=(
            P("section", None, "dp", None),
            P(None, "dp", None),
            P("section", "dp", None),
            P("section", "dp", None),
            P("section", "dp", None),
            P("section", None),
            P(),
        ),
        out_specs=(
            P("section", None, "dp", None),
            P("section", "dp", None),
            P("section", "dp", None),
            P("section", "dp", None),
            P("section", None),
        ),
        check_vma=False,
    )
```

profile of v0, /device:TPU:2, one launch (start us, length us, event | category | flops | bytes accessed | tf_op | source)
XLA Modules:
  0.0 1220.3 jit_solution(14955202066246153748)
XLA Ops:
  10.1 80.4 %all-gather.6.cloned.1.call-done = bf16[1,2,64,4096]{3,1,0,2:T(2,128)(2,1)} async-done(((bf16[1,2,1,4096]{3,1,0,2:T(2,128)(2,1)}), bf16[1,2,64,4096]{3,1,0,2:T(2,128)(2,1)}) %all-gather.6.cloned.1.call-update) | async-done | bytes 1048592 | tf_op jit(solution)/shard_map/all_gather | solution.py:75
  97.3 71.2 %all-gather.4.cloned.1.call-done = bf16[2,64,4096]{2,0,1:T(2,128)(2,1)} async-done(((bf16[2,1,4096]{2,0,1:T(2,128)(2,1)}), bf16[2,64,4096]{2,0,1:T(2,128)(2,1)}) %all-gather.4.cloned.1.call-update) | async-done | bytes 1048592 | tf_op jit(solution)/shard_map/all_gather | solution.py:73
  168.5 9.9 constant_dynamic-slice_fusion.1
  187.0 2.9 fusion.147
  189.8 177.9 %all-reduce.6.cloned.1.call-done = f32[64,4096]{1,0:T(8,128)} async-done(((f32[64,4096]{1,0:T(8,128)}), f32[64,4096]{1,0:T(8,128)}) %all-reduce.6.cloned.1.call-update) | async-done | bytes 1048592 | tf_op jit(solution)/shard_map/psum | solution.py:103
  370.1 2.6 fusion.43
  372.7 2.6 collective-permute-start
  375.4 2.6 fusion.88
  380.2 5.8 collective-permute-done
  393.9 4.5 convolution_add_fusion.5
  398.4 177.5 %all-reduce.8.cloned.1.call-done = f32[64,4096]{1,0:T(8,128)} async-done(((f32[64,4096]{1,0:T(8,128)}), f32[64,4096]{1,0:T(8,128)}) %all-reduce.8.cloned.1.call-update) | async-done | bytes 1048592 | tf_op jit(solution)/shard_map/psum | solution.py:103
  579.8 2.6 collective-permute-start.1
  582.5 4.8 convolution_add_fusion.9
  587.3 2.5 convolution_add_fusion.1
  589.8 3.5 collective-permute-done.1
  600.6 4.5 convolution_add_fusion.4
  605.1 178.0 %all-reduce.10.cloned.1.call-done = f32[64,4096]{1,0:T(8,128)} async-done(((f32[64,4096]{1,0:T(8,128)}), f32[64,4096]{1,0:T(8,128)}) %all-reduce.10.cloned.1.call-update) | async-done | bytes 1048592 | tf_op jit(solution)/shard_map/psum | solution.py:103
  787.8 2.6 collective-permute-start.2
  790.4 4.6 convolution_add_fusion.8
  798.0 3.5 collective-permute-done.2
  809.1 4.7 convolution_add_fusion.3
  813.8 2.6 convolution_add_fusion.7
  816.3 178.0 %all-reduce.12.cloned.1.call-done = f32[64,4096]{1,0:T(8,128)} async-done(((f32[64,4096]{1,0:T(8,128)}), f32[64,4096]{1,0:T(8,128)}) %all-reduce.12.cloned.1.call-update) | async-done | bytes 1048592 | tf_op jit(solution)/shard_map/psum | solution.py:103
  999.1 2.6 collective-permute-start.3
  1001.7 2.5 fusion.143
  1006.4 6.3 collective-permute-done.3
  1016.4 2.6 fusion.145
  1022.0 4.1 fusion.6
  1026.1 2.8 fusion.7
  1029.0 4.1 fusion.5
  1033.1 174.6 %all-reduce.14.cloned.1.call-done = f32[64,4096]{1,0:T(8,128)} async-done(((f32[64,4096]{1,0:T(8,128)}), f32[64,4096]{1,0:T(8,128)}) %all-reduce.14.cloned.1.call-update) | async-done | bytes 1048592 | tf_op jit(solution)/shard_map/psum | solution.py:103
  1209.8 2.8 fusion.153
  (184 shorter events, 73.6 us)
Async XLA Ops:
  7.2 87.8 %copy-start = (bf16[1,224,4096]{2,1,0:T(8,128)(2,1)S(1)}, bf16[1,224,4096]{2,1,0:T(8,128)(2,1)}, u32[]{:S(2)}) copy-start(bf16[1,224,4096]{2,1,0:T(8,128)(2,1)} %param.9) | copy-start | bytes 5505028
  7.2 83.4 %all-gather.6.cloned.1.call-start = ((), (), s32[]{:S(2)}) async-start(), calls=%async_computation.6 | async-start | bytes 1064960 | tf_op jit(solution)/shard_map/all_gather | solution.py:75
  7.9 160.6 %all-gather.4.cloned.1.call-start = ((), (), s32[]{:S(2)}) async-start(), calls=%async_computation | async-start | bytes 1064960 | tf_op jit(solution)/shard_map/all_gather | solution.py:73
  10.1 357.7 %all-reduce.6.cloned.1.call-start = ((), (), s32[]{:S(2)}) async-start(), calls=%async_computation.1 | async-start | bytes 2097152 | tf_op jit(solution)/shard_map/psum | solution.py:103
  97.3 89.6 %copy-start.29 = (f32[2,64,224]{2,1,0:T(8,128)}, f32[2,64,224]{2,1,0:T(8,128)S(1)}, u32[]{:S(2)}) copy-start(f32[2,64,224]{2,1,0:T(8,128)S(1)} %fusion.23) | copy-start | bytes 344068
  168.5 10.0 copy-start.12
  182.3 393.6 %all-reduce.8.cloned.1.call-start = ((), (), s32[]{:S(2)}) async-start(), calls=%async_computation.2 | async-start | bytes 2097152 | tf_op jit(solution)/shard_map/psum | solution.py:103
  187.0 191.0 %copy-start.58 = (f32[64]{0:T(128)}, f32[64]{0:T(128)S(1)}, u32[]{:S(2)}) copy-start(f32[64]{0:T(128)S(1)} %get-tuple-element.16) | copy-start | bytes 772
  187.0 180.8 %copy-start.35 = (f32[1,4096]{1,0:T(1,128)S(1)}, f32[1,4096]{1,0:T(1,128)}, u32[]{:S(2)}) copy-start(f32[1,4096]{1,0:T(1,128)} %param.12) | copy-start | bytes 49156
  372.7 13.2 %collective-permute-start = (bf16[64,4096]{1,0:T(8,128)(2,1)S(1)}, bf16[64,4096]{1,0:T(8,128)(2,1)S(1)}, u32[]{:S(2)}, u32[]{:S(2)}) collective-permute-start(bf16[64,4096]{1,0:T(8,128)(2,1)S(1)} %fusion.43), channel_id=1, source_target_pairs={{1,0},{2,1},{3,2},{5,4},{6,5},{7,6},{9,8},{10,9},{11,10},{13,12},{... | collective-permute-start | bytes 1572872 | tf_op jit(solution)/shard_map/ppermute | solution.py:10
  377.9 8.0 copy-start.28
  379.1 7.5 copy-start.13
  379.1 7.5 copy-start.30
  390.4 392.7 %all-reduce.10.cloned.1.call-start = ((), (), s32[]{:S(2)}) async-start(), calls=%async_computation.3 | async-start | bytes 2097152 | tf_op jit(solution)/shard_map/psum | solution.py:103
  579.8 7.4 copy-start.37
  579.8 7.4 copy-start.31
  579.8 13.4 %collective-permute-start.1 = (bf16[64,4096]{1,0:T(8,128)(2,1)S(1)}, bf16[64,4096]{1,0:T(8,128)(2,1)S(1)}, u32[]{:S(2)}, u32[]{:S(2)}) collective-permute-start(bf16[64,4096]{1,0:T(8,128)(2,1)S(1)} %fusion.50), channel_id=1, source_target_pairs={{1,0},{2,1},{3,2},{5,4},{6,5},{7,6},{9,8},{10,9},{11,10},{13,12},{... | collective-permute-start | bytes 1572872 | tf_op jit(solution)/shard_map/ppermute | solution.py:10
  593.9 191.6 %copy-start.23 = (bf16[64,4096]{1,0:T(8,128)(2,1)}, bf16[64,4096]{1,0:T(8,128)(2,1)S(1)}, u32[]{:S(2)}) copy-start(bf16[64,4096]{1,0:T(8,128)(2,1)S(1)} %fusion.73) | copy-start | bytes 1572868
  597.6 396.7 %all-reduce.12.cloned.1.call-start = ((), (), s32[]{:S(2)}) async-start(), calls=%async_computation.4 | async-start | bytes 2097152 | tf_op jit(solution)/shard_map/psum | solution.py:103
  783.1 7.3 copy-start.46
  787.8 7.2 copy-start.39
  787.8 13.6 %collective-permute-start.2 = (bf16[64,4096]{1,0:T(8,128)(2,1)}, bf16[64,4096]{1,0:T(8,128)(2,1)S(1)}, u32[]{:S(2)}, u32[]{:S(2)}) collective-permute-start(bf16[64,4096]{1,0:T(8,128)(2,1)} %fusion.57), channel_id=1, source_target_pairs={{1,0},{2,1},{3,2},{5,4},{6,5},{7,6},{9,8},{10,9},{11,10},{13,12},{... | collective-permute-start | bytes 1572872 | tf_op jit(solution)/shard_map/ppermute | solution.py:10
  808.8 398.8 %all-reduce.14.cloned.1.call-start = ((), (), s32[]{:S(2)}) async-start(), calls=%async_computation.5 | async-start | bytes 2097152 | tf_op jit(solution)/shard_map/psum | solution.py:103
  994.3 7.3 copy-start.32
  999.1 13.7 %collective-permute-start.3 = (bf16[64,4096]{1,0:T(8,128)(2,1)}, bf16[64,4096]{1,0:T(8,128)(2,1)}, u32[]{:S(2)}, u32[]{:S(2)}) collective-permute-start(bf16[64,4096]{1,0:T(8,128)(2,1)} %fusion.64), channel_id=1, source_target_pairs={{1,0},{2,1},{3,2},{5,4},{6,5},{7,6},{9,8},{10,9},{11,10},{13,12},{... | collective-permute-start | bytes 1572872 | tf_op jit(solution)/shard_map/ppermute | solution.py:10
  1006.4 8.4 copy-start.16
  1029.0 178.7 %copy-start.11 = (bf16[1,2,64,4096]{3,2,1,0:T(8,128)(2,1)S(1)}, bf16[1,2,64,4096]{3,2,1,0:T(8,128)(2,1)}, u32[]{:S(2)}) copy-start(bf16[1,2,64,4096]{3,2,1,0:T(8,128)(2,1)} %copy.28) | copy-start | bytes 3145732
  1033.0 176.8 %copy-start.41 = (bf16[2,1,4096]{2,0,1:T(2,128)(2,1)S(1)}, bf16[2,1,4096]{2,0,1:T(2,128)(2,1)}, u32[]{:S(2)}) copy-start(bf16[2,1,4096]{2,0,1:T(2,128)(2,1)} %dynamic_update_slice.20) | copy-start | bytes 49156
  1033.0 179.8 %copy-start.54 = (f32[4096]{0:T(1024)S(1)}, f32[4096]{0:T(1024)}, u32[]{:S(2)}) copy-start(f32[4096]{0:T(1024)} %get-tuple-element.7) | copy-start | bytes 49156
  1033.0 179.8 %copy-start.55 = (f32[4096]{0:T(1024)S(1)}, f32[4096]{0:T(1024)}, u32[]{:S(2)}) copy-start(f32[4096]{0:T(1024)} %get-tuple-element.5) | copy-start | bytes 49156
  1033.0 179.8 %copy-start.56 = (f32[4096]{0:T(1024)S(1)}, f32[4096]{0:T(1024)}, u32[]{:S(2)}) copy-start(f32[4096]{0:T(1024)} %get-tuple-element.9) | copy-start | bytes 49156
  1033.0 179.8 %copy-start.57 = (f32[4096]{0:T(1024)S(1)}, f32[4096]{0:T(1024)}, u32[]{:S(2)}) copy-start(f32[4096]{0:T(1024)} %get-tuple-element.11) | copy-start | bytes 49156
  (38 other events, 107.2 us)
Sparse Core Ops, SparseCore 0:
  10.8 79.7 all-gather.5
  93.9 74.5 all-gather.3
  182.4 185.2 all-reduce.5
  390.5 185.3 all-reduce.7
  597.7 185.3 all-reduce.9
  808.9 185.3 all-reduce.11
  1022.1 185.4 all-reduce.13
where the time goes:
time: 1220 us
  waiting for transfers between devices  1060 us (87%)
  matrix products  68.6 us (6%)
  other arithmetic  42.1 us (3%)
  local copies, waits for them, and re-layouts  26.6 us (2%)
  between operations  14.8 us (1%)
    psum x5, waiting for transfers between devices, on_device(): grad_normed = lax.psum(partial_sum, 'dp')  886 us
    all_gather x1, waiting for transfers between devices, on_device(): gathered_all = lax.all_gather(layer_rows, 'dp', axis=1, tiled=True)  80.4 us
    all_gather x1, waiting for transfers between devices, on_device(): top_whole = lax.all_gather(top_local, 'dp', axis=1, tiled=True)  71.2 us
    dot_general x15, matrix products, transposed_product(): lax.dot_general(left_rows, right_rows, (((0,), (0,)), ((), ())), preferre...  52.1 us
  transfers between devices with their start and end apart: 11, of which 11 were waited for; matrix products, arithmetic and copies ran while one was open for 6% of the time, Pallas kernels for 0%

commit v1 on v0

--- a/solution.py
+++ b/solution.py
@@ -100,7 +100,7 @@
         partial_sum = jnp.dot(grad_gate, gate_mat, preferred_element_type=jnp.float32) + jnp.dot(
             grad_up, up_mat, preferred_element_type=jnp.float32
         )
-        grad_normed = lax.psum(partial_sum, "dp")
+        grad_normed = jnp.sum(lax.all_gather(partial_sum, "dp"), axis=0)
         grad_full = norm_back(gathered, full_inv, full_up, grad_normed, gain_row)
         gain_total = gain_total + jnp.sum(
             grad_normed * gathered.astype(jnp.float32) * full_inv, axis=0

time: 1220 us -> 1580 us (1.30)
  waiting for transfers between devices: 1060 us -> 1310 us
  other arithmetic: 42.1 us -> 154 us
    all_gather x0 -> x5, waiting for transfers between devices: none -> 1100 us  [on_device(): grad_normed = jnp.sum(lax.all_gather(partial_sum, 'dp'), axis=0)]
    psum x5 -> x0, waiting for transfers between devices: 886 us -> none  [on_device(): grad_normed = lax.psum(partial_sum, 'dp')]
    reduce_sum x0 -> x5, other arithmetic: none -> 108 us  [on_device(): grad_normed = jnp.sum(lax.all_gather(partial_sum, 'dp'), axis=0)]
    ppermute x4, waiting for transfers between devices: 19 us -> 54.5 us  [from_behind(): return lax.ppermute(x, axis, pairs)]
  transfers between devices with their start and end apart: 11 -> 11, of which waited for: 11 -> 11; matrix products, arithmetic and copies ran while one was open for 6% -> 4% of each run, Pallas kernels for 0% -> 0%
where the time goes in v1:
time: 1580 us
  waiting for transfers between devices  1310 us (83%)
  other arithmetic  154 us (10%)
  matrix products  58.3 us (4%)
  local copies, waits for them, and re-layouts  30.5 us (2%)
    all_gather x5, waiting for transfers between devices, on_device(): grad_normed = jnp.sum(lax.all_gather(partial_sum, 'dp'), axis=0)  1100 us
    reduce_sum x5, other arithmetic, on_device(): grad_normed = jnp.sum(lax.all_gather(partial_sum, 'dp'), axis=0)  108 us
    all_gather x1, waiting for transfers between devices, on_device(): gathered_all = lax.all_gather(layer_rows, 'dp', axis=1, tiled=True)  80.4 us
    all_gather x1, waiting for transfers between devices, on_device(): top_whole = lax.all_gather(top_local, 'dp', axis=1, tiled=True)  71.7 us
    ppermute x4, waiting for transfers between devices, from_behind(): return lax.ppermute(x, axis, pairs)  54.5 us
    dot_general x15, matrix products, transposed_product(): lax.dot_general(left_rows, right_rows, (((0,), (0,)), ((), ())), preferre...  42.7 us
  transfers between devices with their start and end apart: 11, of which 11 were waited for; matrix products, arithmetic and copies ran while one was open for 4% of the time, Pallas kernels for 0%

profile of v1, /device:TPU:2, one launch (start us, length us, event | category | flops | bytes accessed | tf_op | source)
XLA Modules:
  0.0 1577.9 jit_solution(7232983707224274253)
XLA Ops:
  10.1 80.4 %all-gather.16.cloned.1.call-done = bf16[1,2,64,4096]{3,1,0,2:T(2,128)(2,1)} async-done(((bf16[1,2,1,4096]{3,1,0,2:T(2,128)(2,1)}), bf16[1,2,64,4096]{3,1,0,2:T(2,128)(2,1)}) %all-gather.16.cloned.1.call-update) | async-done | bytes 1048592 | tf_op jit(solution)/shard_map/all_gather | solution.py:75
  96.7 71.7 %all-gather.14.cloned.1.call-done = bf16[2,64,4096]{2,0,1:T(2,128)(2,1)} async-done(((bf16[2,1,4096]{2,0,1:T(2,128)(2,1)}), bf16[2,64,4096]{2,0,1:T(2,128)(2,1)}) %all-gather.14.cloned.1.call-update) | async-done | bytes 1048592 | tf_op jit(solution)/shard_map/all_gather | solution.py:73
  168.5 10.1 constant_dynamic-slice_fusion.1
  182.6 2.8 copy.33
  186.0 230.4 %all-gather.18.cloned.1.call-done = f32[4096,4096]{1,0:T(8,128)} async-done(((f32[64,4096]{1,0:T(8,128)}), f32[4096,4096]{1,0:T(8,128)}) %all-gather.18.cloned.1.call-update) | async-done | bytes 67108880 | tf_op jit(solution)/shard_map/all_gather | solution.py:103
  416.4 21.7 %reduce_sum.145 = f32[64,4096]{1,0:T(8,128)} reduce(f32[64,64,4096]{2,1,0:T(8,128)} %bitcast.13, f32[]{:T(128)} %constant.130.clone.1), dimensions={0}, to_apply=%region_1.2 | reduce | flops 16515072 | bytes 68157440 | tf_op jit(solution)/shard_map/reduce_sum | solution.py:103
  440.4 2.5 fusion.43
  442.9 2.6 collective-permute-start
  445.6 13.4 collective-permute-done
  465.6 233.1 %all-gather.20.cloned.1.call-done = f32[4096,4096]{1,0:T(8,128)} async-done(((f32[64,4096]{1,0:T(8,128)}), f32[4096,4096]{1,0:T(8,128)}) %all-gather.20.cloned.1.call-update) | async-done | bytes 67108880 | tf_op jit(solution)/shard_map/all_gather | solution.py:103
  698.7 21.7 %reduce_sum.147 = f32[64,4096]{1,0:T(8,128)} reduce(f32[64,64,4096]{2,1,0:T(8,128)} %bitcast.21, f32[]{:T(128)} %constant.130.clone.1), dimensions={0}, to_apply=%region_3.4 | reduce | flops 16515072 | bytes 68157440 | tf_op jit(solution)/shard_map/reduce_sum | solution.py:103
  727.5 13.8 collective-permute-done.1
  747.1 233.1 %all-gather.22.cloned.1.call-done = f32[4096,4096]{1,0:T(8,128)} async-done(((f32[64,4096]{1,0:T(8,128)}), f32[4096,4096]{1,0:T(8,128)}) %all-gather.22.cloned.1.call-update) | async-done | bytes 67108880 | tf_op jit(solution)/shard_map/all_gather | solution.py:103
  980.2 21.7 %reduce_sum.149 = f32[64,4096]{1,0:T(8,128)} reduce(f32[64,64,4096]{2,1,0:T(8,128)} %bitcast.30, f32[]{:T(128)} %constant.130.clone.1), dimensions={0}, to_apply=%region_5.6 | reduce | flops 16515072 | bytes 68157440 | tf_op jit(solution)/shard_map/reduce_sum | solution.py:103
  1009.0 13.8 collective-permute-done.2
  1028.6 233.1 %all-gather.24.cloned.1.call-done = f32[4096,4096]{1,0:T(8,128)} async-done(((f32[64,4096]{1,0:T(8,128)}), f32[4096,4096]{1,0:T(8,128)}) %all-gather.24.cloned.1.call-update) | async-done | bytes 67108880 | tf_op jit(solution)/shard_map/all_gather | solution.py:103
  1261.7 21.7 %reduce_sum.151 = f32[64,4096]{1,0:T(8,128)} reduce(f32[64,64,4096]{2,1,0:T(8,128)} %bitcast.39, f32[]{:T(128)} %constant.130.clone.1), dimensions={0}, to_apply=%region_7.8 | reduce | flops 16515072 | bytes 68157440 | tf_op jit(solution)/shard_map/reduce_sum | solution.py:103
  1288.1 2.7 collective-permute-start.3
  1290.8 13.6 collective-permute-done.3
  1312.7 3.2 fusion.88
  1318.4 2.9 fusion.147
  1325.8 4.7 convolution_add_fusion.9
  1330.6 2.5 convolution_add_fusion.5
  1333.9 2.5 convolution_add_fusion.1
  1338.7 4.7 convolution_add_fusion.8
  1343.5 2.6 convolution_add_fusion.4
  1349.0 3.4 fusion.143
  1355.6 2.6 convolution_add_fusion.3
  1359.8 4.1 fusion.7
  1370.2 173.1 %all-gather.26.cloned.1.call-done = f32[4096,4096]{1,0:T(8,128)} async-done(((f32[64,4096]{1,0:T(8,128)}), f32[4096,4096]{1,0:T(8,128)}) %all-gather.26.cloned.1.call-update) | async-done | bytes 67108880 | tf_op jit(solution)/shard_map/all_gather | solution.py:103
  1543.3 21.7 %reduce_sum.153 = f32[64,4096]{1,0:T(8,128)} reduce(f32[64,64,4096]{2,1,0:T(8,128)} %bitcast.49, f32[]{:T(128)} %constant.130.clone.1), dimensions={0}, to_apply=%region_9.10 | reduce | flops 16515072 | bytes 68157440 | tf_op jit(solution)/shard_map/reduce_sum | solution.py:103
  1567.3 3.0 fusion.153
  (215 shorter events, 88.3 us)
Async XLA Ops:
  7.2 88.0 %copy-start = (bf16[1,224,4096]{2,1,0:T(8,128)(2,1)S(1)}, bf16[1,224,4096]{2,1,0:T(8,128)(2,1)}, u32[]{:S(2)}) copy-start(bf16[1,224,4096]{2,1,0:T(8,128)(2,1)} %param.9) | copy-start | bytes 5505028
  7.2 83.4 %all-gather.16.cloned.1.call-start = ((), (), s32[]{:S(2)}) async-start(), calls=%async_computation.1 | async-start | bytes 1064960 | tf_op jit(solution)/shard_map/all_gather | solution.py:75
  7.9 160.6 %all-gather.14.cloned.1.call-start = ((), (), s32[]{:S(2)}) async-start(), calls=%async_computation | async-start | bytes 1064960 | tf_op jit(solution)/shard_map/all_gather | solution.py:73
  10.1 406.4 %all-gather.18.cloned.1.call-start = ((), (), s32[]{:S(2)}) async-start(), calls=%async_computation.2 | async-start | bytes 68157440 | tf_op jit(solution)/shard_map/all_gather | solution.py:103
  96.7 81.9 %copy-start.34 = (f32[2,64,224]{2,1,0:T(8,128)}, f32[2,64,224]{2,1,0:T(8,128)S(1)}, u32[]{:S(2)}) copy-start(f32[2,64,224]{2,1,0:T(8,128)S(1)} %fusion.23) | copy-start | bytes 344068
  168.5 10.1 copy-start.9
  182.6 516.2 %all-gather.20.cloned.1.call-start = ((), (), s32[]{:S(2)}) async-start(), calls=%async_computation.3 | async-start | bytes 68157440 | tf_op jit(solution)/shard_map/all_gather | solution.py:103
  186.0 252.1 %copy-start.70 = (f32[64]{0:T(128)}, f32[64]{0:T(128)S(1)}, u32[]{:S(2)}) copy-start(f32[64]{0:T(128)S(1)} %get-tuple-element.48) | copy-start | bytes 772
  416.4 21.7 %copy-start.41 = (f32[1,4096]{1,0:T(1,128)S(1)}, f32[1,4096]{1,0:T(1,128)}, u32[]{:S(2)}) copy-start(f32[1,4096]{1,0:T(1,128)} %param.12) | copy-start | bytes 49156
  442.9 16.1 %copy-start.42 = (bf16[64,4096]{1,0:T(8,128)(2,1)}, bf16[64,4096]{1,0:T(8,128)(2,1)S(1)}, u32[]{:S(2)}) copy-start(bf16[64,4096]{1,0:T(8,128)(2,1)S(1)} %fusion.43) | copy-start | bytes 1572868
  442.9 16.1 %collective-permute-start = (bf16[64,4096]{1,0:T(8,128)(2,1)S(1)}, bf16[64,4096]{1,0:T(8,128)(2,1)}, u32[]{:S(2)}, u32[]{:S(2)}) collective-permute-start(bf16[64,4096]{1,0:T(8,128)(2,1)S(1)} %fusion.43), channel_id=1, source_target_pairs={{1,0},{2,1},{3,2},{5,4},{6,5},{7,6},{9,8},{10,9},{11,10},{13,12},{... | collective-permute-start | bytes 1572872 | tf_op jit(solution)/shard_map/ppermute | solution.py:10
  445.6 15.4 copy-start.10
  465.6 514.6 %all-gather.22.cloned.1.call-start = ((), (), s32[]{:S(2)}) async-start(), calls=%async_computation.4 | async-start | bytes 68157440 | tf_op jit(solution)/shard_map/all_gather | solution.py:103
  725.0 16.3 %collective-permute-start.1 = (bf16[64,4096]{1,0:T(8,128)(2,1)}, bf16[64,4096]{1,0:T(8,128)(2,1)}, u32[]{:S(2)}, u32[]{:S(2)}) collective-permute-start(bf16[64,4096]{1,0:T(8,128)(2,1)} %fusion.50), channel_id=1, source_target_pairs={{1,0},{2,1},{3,2},{5,4},{6,5},{7,6},{9,8},{10,9},{11,10},{13,12},{... | collective-permute-start | bytes 1572872 | tf_op jit(solution)/shard_map/ppermute | solution.py:10
  727.5 15.8 %copy-start.11 = (bf16[1,224,4096]{2,1,0:T(8,128)(2,1)S(1)}, bf16[1,224,4096]{2,1,0:T(8,128)(2,1)}, u32[]{:S(2)}) copy-start(bf16[1,224,4096]{2,1,0:T(8,128)(2,1)} %param.11) | copy-start | bytes 5505028
  727.5 15.8 %copy-start.35 = (f32[2,64,224]{2,1,0:T(8,128)S(1)}, f32[2,64,224]{2,1,0:T(8,128)}, u32[]{:S(2)}) copy-start(f32[2,64,224]{2,1,0:T(8,128)} %copy-done.34) | copy-start | bytes 344068
  747.1 514.7 %all-gather.24.cloned.1.call-start = ((), (), s32[]{:S(2)}) async-start(), calls=%async_computation.5 | async-start | bytes 68157440 | tf_op jit(solution)/shard_map/all_gather | solution.py:103
  1006.6 16.3 %collective-permute-start.2 = (bf16[64,4096]{1,0:T(8,128)(2,1)}, bf16[64,4096]{1,0:T(8,128)(2,1)}, u32[]{:S(2)}, u32[]{:S(2)}) collective-permute-start(bf16[64,4096]{1,0:T(8,128)(2,1)} %fusion.57), channel_id=1, source_target_pairs={{1,0},{2,1},{3,2},{5,4},{6,5},{7,6},{9,8},{10,9},{11,10},{13,12},{... | collective-permute-start | bytes 1572872 | tf_op jit(solution)/shard_map/ppermute | solution.py:10
  1009.0 15.8 %copy-start.12 = (bf16[1,224,4096]{2,1,0:T(8,128)(2,1)S(1)}, bf16[1,224,4096]{2,1,0:T(8,128)(2,1)}, u32[]{:S(2)}) copy-start(bf16[1,224,4096]{2,1,0:T(8,128)(2,1)} %param.11) | copy-start | bytes 5505028
  1009.0 15.8 %copy-start.36 = (f32[2,64,224]{2,1,0:T(8,128)S(1)}, f32[2,64,224]{2,1,0:T(8,128)}, u32[]{:S(2)}) copy-start(f32[2,64,224]{2,1,0:T(8,128)} %copy-done.34) | copy-start | bytes 344068
  1028.6 514.7 %all-gather.26.cloned.1.call-start = ((), (), s32[]{:S(2)}) async-start(), calls=%async_computation.6 | async-start | bytes 68157440 | tf_op jit(solution)/shard_map/all_gather | solution.py:103
  1288.1 16.3 %collective-permute-start.3 = (bf16[64,4096]{1,0:T(8,128)(2,1)}, bf16[64,4096]{1,0:T(8,128)(2,1)}, u32[]{:S(2)}, u32[]{:S(2)}) collective-permute-start(bf16[64,4096]{1,0:T(8,128)(2,1)} %fusion.64), channel_id=1, source_target_pairs={{1,0},{2,1},{3,2},{5,4},{6,5},{7,6},{9,8},{10,9},{11,10},{13,12},{... | collective-permute-start | bytes 1572872 | tf_op jit(solution)/shard_map/ppermute | solution.py:10
  1290.8 15.6 copy-start.13
  1290.8 15.6 copy-start.37
  1338.7 4.7 copy-start.53
  1343.5 5.5 copy-start.27
  1543.3 21.7 %copy-start.8 = (bf16[1,2,64,4096]{3,2,1,0:T(8,128)(2,1)S(1)}, bf16[1,2,64,4096]{3,2,1,0:T(8,128)(2,1)}, u32[]{:S(2)}) copy-start(bf16[1,2,64,4096]{3,2,1,0:T(8,128)(2,1)} %copy.33) | copy-start | bytes 3145732
  1543.3 21.7 %copy-start.71 = (f32[64]{0:T(128)S(1)}, f32[64]{0:T(128)}, u32[]{:S(2)}) copy-start(f32[64]{0:T(128)} %get-tuple-element.16) | copy-start | bytes 772
  1565.0 5.4 copy-start.66
  1565.0 5.4 copy-start.67
  1565.0 5.4 copy-start.68
  1565.0 5.4 copy-start.69
  (51 other events, 116.3 us)
Sparse Core Ops, SparseCore 0:
  10.8 79.7 all-gather.15
  93.9 74.5 all-gather.13
  182.7 233.6 all-gather.17
  465.7 232.9 all-gather.19
  747.2 232.9 all-gather.21
  1028.7 232.9 all-gather.23
  1310.3 232.9 all-gather.25
